TPU v7x, 32 devices: a whole 2x2x4 slice. The times are simulated.
32 devices in a mesh: groups: 2 (over x), wide: 16 (over z, y, core).
Axes of the slice: x: 2, y: 2, z: 4, core: 2. Of those that a mesh axis runs over, the one named last changes fastest.
Arguments:
- queries: bfloat16 [32, 16, 8, 128], P(('groups', 'wide')), parts along dimension 0, may hold values from -250 to 250
- keys_cache: bfloat16 [32, 16, 320, 128], P(('groups', 'wide')), parts along dimension 0, may hold values from -6 to 6
- values_cache: bfloat16 [32, 16, 320, 128], P(('groups', 'wide')), parts along dimension 0, may hold values from -6 to 6
- new_keys: bfloat16 [32, 16, 128], P(('groups', 'wide')), parts along dimension 0, may hold values from -6 to 6
- new_values: bfloat16 [32, 16, 128], P(('groups', 'wide')), parts along dimension 0, may hold values from -6 to 6
- lengths: int32 [64], P('groups'), parts along dimension 0, may hold values from 1 to 320, as said below
- assignment: int32 [64], P('groups'), parts along dimension 0, may hold values from 0 to 31, each once
- residual: bfloat16 [64, 8192], P('groups', 'wide'), parts along dimension 0, may hold values from -6 to 6
- w_out: bfloat16 [8192, 8192], P('wide'), may hold values from -0.0625 to 0.0625
- w_gate: bfloat16 [20480, 8192], P('wide'), may hold values from -0.0625 to 0.0625
- w_up: bfloat16 [20480, 8192], P('wide'), may hold values from -0.0625 to 0.0625
- w_down: bfloat16 [20480, 8192], P('wide'), may hold values from -0.0625 to 0.0625
- norm_gain: float32 [8192], P('wide'), may hold values from 0.25 to 1.75
Outputs:
- mixed: bfloat16 [64, 8192], P('groups', 'wide'), parts along dimension 0
There are 2 independent parts, one for each index of `groups`. A program takes and returns all parts, laid end to end along the dimension named above; an argument that names none is the same for every part. Nothing has to cross between parts.
Inputs may be any that keep to these rules, and one draw needn't show every extreme that they name: `lengths`: every length is at least 1; one cache row has length exactly 320 in every draw. `assignment`: A permutation of the request numbers.
All inputs are finite; a program needn't handle non-finite values.
Results may differ from a plain program's by a relative error of at most 0.0052.
Values may be sent and summed in bfloat16 or wider, within the bound.
A program may use at most 128 MiB of HBM per device.

v0:
```python
import math

import jax
import jax.numpy as jnp
from jax import lax
from jax.sharding import PartitionSpec as P

D = 8192
KV = 8


KEY_BLOCK = 64
EPSILON = 1e-05
NEG_FILL = -1e30


def contract_last(left, right):
    return lax.dot_general(
        left, right, (((1,), (1,)), ((), ())), preferred_element_type=jnp.float32
    )


def masked_scores(query_rows, keys_local, lens_local, block_index, inv_scale):
    key_block = lax.dynamic_slice_in_dim(keys_local, block_index * KEY_BLOCK, KEY_BLOCK, 1)
    scores = (
        jnp.einsum("rqe,rpe->rqp", query_rows, key_block, preferred_element_type=jnp.float32)
        * inv_scale
    )
    position = block_index * KEY_BLOCK + lax.broadcasted_iota(jnp.int32, scores.shape, 2)
    return jnp.where(position < lens_local[:, None, None], scores, NEG_FILL)


def on_device(
    queries,
    keys_cache,
    values_cache,
    new_keys,
    new_values,
    lengths,
    assignment,
    residual,
    w_out,
    w_gate,
    w_up,
    w_down,
    norm_gain,
):
    my_index = lax.axis_index("wide")
    my_shard = my_index // KV
    req_dev = queries.shape[1]
    query_rows = queries[0]
    keys_local = keys_cache[0]
    values_local = values_cache[0]
    lens_local = lax.dynamic_slice_in_dim(lengths, my_shard * req_dev, req_dev)
    inv_scale = 1.0 / math.sqrt(query_rows.shape[2])
    own_score = (
        jnp.einsum("rqe,re->rq", query_rows, new_keys[0], preferred_element_type=jnp.float32)
        * inv_scale
    )
    block_count = (jnp.max(lens_local) + KEY_BLOCK - 1) // KEY_BLOCK

    def find_top(block_index, running):
        return jnp.maximum(
            running,
            jnp.max(
                masked_scores(query_rows, keys_local, lens_local, block_index, inv_scale), axis=2
            ),
        )

    top_score = lax.fori_loop(0, block_count, find_top, own_score)
    own_weight = jnp.exp(own_score - top_score)
    own_low = lax.optimization_barrier(own_weight.astype(jnp.bfloat16)).astype(jnp.float32)
    start_state = (own_weight, own_low[:, :, None] * new_values[0].astype(jnp.float32)[:, None, :])

    def accumulate(block_index, state_pair):
        total_sum, weighted = state_pair
        weights = jnp.exp(
            masked_scores(query_rows, keys_local, lens_local, block_index, inv_scale)
            - top_score[:, :, None]
        )
        value_block = lax.dynamic_slice_in_dim(values_local, block_index * KEY_BLOCK, KEY_BLOCK, 1)
        weighted = weighted + jnp.einsum(
            "rqp,rpe->rqe",
            weights.astype(jnp.bfloat16),
            value_block,
            preferred_element_type=jnp.float32,
        )
        return (total_sum + jnp.sum(weights, axis=2), weighted)

    total_sum, weighted = lax.fori_loop(0, block_count, accumulate, start_state)
    attended = (weighted / total_sum[:, :, None]).astype(jnp.bfloat16).reshape(1, req_dev, -1)
    feat_width = attended.shape[2]
    head_piece = lax.all_gather(attended, "wide", axis=0, tiled=True)

    def one_source(offset, running):
        source_shard = offset // KV
        source_group = offset % KV
        request_ids = lax.dynamic_slice_in_dim(assignment, source_shard * req_dev, req_dev)
        out_cols = lax.dynamic_slice_in_dim(w_out, source_group * feat_width, feat_width, 1)
        source_rows = lax.dynamic_index_in_dim(head_piece, offset, 0, keepdims=False)
        term = contract_last(source_rows, out_cols)
        return running.at[request_ids].add(term)

    projected = lax.fori_loop(
        0,
        head_piece.shape[0],
        one_source,
        jnp.zeros((assignment.shape[0], w_out.shape[0]), jnp.float32),
    )
    hidden_state = residual.astype(jnp.float32) + projected
    row_squares = lax.psum(jnp.sum(hidden_state * hidden_state, axis=1), "wide")
    inv_rms = lax.rsqrt(row_squares / D + EPSILON)
    normed_cols = (hidden_state * inv_rms[:, None] * norm_gain[None, :]).astype(jnp.bfloat16)
    normed_piece = lax.all_gather(normed_cols, "wide", axis=1, tiled=True)
    gate_val = contract_last(normed_piece, w_gate)
    up_val = contract_last(normed_piece, w_up)
    activated = (jax.nn.silu(gate_val) * up_val).astype(jnp.bfloat16)
    down_terms = jnp.dot(activated, w_down, preferred_element_type=jnp.float32)
    down_part = lax.psum_scatter(down_terms, "wide", scatter_dimension=1, tiled=True)
    return (hidden_state + down_part).astype(jnp.bfloat16)


def solution(mesh):
    placed = (
        P(("groups", "wide"), None, None, None),
        P(("groups", "wide"), None, None, None),
        P(("groups", "wide"), None, None, None),
        P(("groups", "wide"), None, None),
        P(("groups", "wide"), None, None),
        P("groups"),
        P("groups"),
        P("groups", "wide"),
        P("wide", None),
        P("wide", None),
        P("wide", None),
        P("wide", None),
        P("wide"),
    )
    return jax.shard_map(
        on_device, mesh=mesh, in_specs=placed, out_specs=P("groups", "wide"), check_vma=False
    )
```

profile of v0, /device:TPU:0, one launch (start us, length us, event | category | flops | bytes accessed | tf_op | source)
XLA Modules:
  0.0 251.5 jit_solution(5730291661640036402)
XLA Ops:
  9.6 6.5 %while.37 = (s32[]{:T(128)}, f32[16,8]{1,0:T(8,128)S(1)}, s32[]{:T(128)}, s32[16]{0:T(128)S(1)}, bf16[16,320,128]{2,1,0:T(8,128)(2,1)}, /*index=5*/bf16[16,8,128...) while((s32[]{:T(128)}, f32[16,8]{1,0:T(8,128)S(1)}, s32[]{:T(128)}, s32[16]{0:T(128)S(1)}, ...), condition=%wide.region_3.4_spmd, body=%wide.region_1.3_spmd.sunk | while | flops 2129990 | bytes 297691 | solution.py:70
  16.9 12.3 %while.38 = (s32[]{:T(128)}, f32[16,8]{1,0:T(8,128)S(1)}, f32[16,8,128]{2,1,0:T(8,128)S(1)}, s32[]{:T(128)}, s32[16]{0:T(128)S(1)}, /*index=5*/bf16[16,320,128]{...) while((s32[]{:T(128)}, f32[16,8]{1,0:T(8,128)S(1)}, ...), condition=%wide.region_6.7_spmd, body=%wide.region_4.6_spmd.sunk | while | flops 4259910 | bytes 724215 | solution.py:90
  29.4 21.5 %all_gather.6 = bf16[16,16,1024]{2,1,0:T(8,128)(2,1)S(1)} all-gather(bf16[1,16,1024]{2,1,0:T(8,128)(2,1)S(1)} %reshape.17), channel_id=1, replica_groups=mesh['groups'=2,'wide'=16] {'wide'}, dimensions={0}, use_global_device_ids=true | all-gather | bytes 557056 | tf_op jit(solution)/shard_map/all_gather | solution.py:93
  50.9 50.0 %while.39 = (s32[]{:T(128)}, f32[32,512]{1,0:T(8,128)S(1)}, s32[32]{0:T(128)}, bf16[16,16,1024]{2,1,0:T(8,128)(2,1)S(1)}, bf16[512,8192]{1,0:T(8,128)(2,1)}, /*i...) while((s32[]{:T(128)}, f32[32,512]{1,0:T(8,128)S(1)}, ...), condition=%wide.region_9.10_spmd, body=%wide.region_7.9_spmd.sunk | while | flops 16785476 | bytes 1212976 | solution.py:104
  51.6 1.6 fusion.56
  54.7 1.6 fusion.56
  57.9 1.6 fusion.56
  61.0 1.6 fusion.56
  67.2 1.6 fusion.56
  73.5 1.6 fusion.56
  76.6 1.6 fusion.56
  79.7 1.6 fusion.56
  82.9 1.6 fusion.56
  86.0 1.6 fusion.56
  89.1 1.6 fusion.56
  92.2 1.6 fusion.56
  95.3 1.6 fusion.56
  98.5 1.6 fusion.56
  101.7 29.8 %psum.7 = f32[32]{0:T(128)S(1)} all-reduce(f32[32]{0:T(128)S(1)} %multiply_reduce_fusion), channel_id=1, replica_groups=mesh['groups'=2,'wide'=16] {'wide'}, use_global_device_ids=true, to_apply=%region_11.12 | all-reduce | flops 32 | bytes 256 | tf_op jit(solution)/shard_map/psum | solution.py:111
  132.4 18.8 %all_gather.7 = bf16[32,8192]{1,0:T(8,128)(2,1)S(1)} all-gather(bf16[32,512]{1,0:T(8,128)(2,1)S(1)} %multiply_convert_fusion), channel_id=1, replica_groups=mesh['groups'=2,'wide'=16] {'wide'}, dimensions={1}, use_global_device_ids=true | all-gather | bytes 557056 | tf_op jit(solution)/shard_map/all_gather | solution.py:114
  151.2 10.4 %fusion.26 = f32[32,1280]{1,0:T(8,128)S(1)} fusion(bf16[32,8192]{1,0:T(8,128)(2,1)S(1)} %all_gather.7, bf16[1280,8192]{1,0:T(8,128)(2,1)} %param.28), kind=kOutput, calls=%fused_computation.44 | convolution fusion | flops 671088640 | bytes 21659648 | tf_op jit(solution)/shard_map/dot_general | solution.py:18
  161.6 10.5 %fusion.19 = bf16[32,1280]{1,0:T(8,128)(2,1)S(1)} fusion(bf16[32,8192]{1,0:T(8,128)(2,1)S(1)} %all_gather.7, bf16[1280,8192]{1,0:T(8,128)(2,1)} %param.29, f32[32,1280]{1,0:T(8,128)S(1)} %fusion.26), kind=kOutput, calls=%fused_computation.27 | convolution fusion | flops 671334400 | bytes 21741568 | tf_op jit(solution)/shard_map/dot_general | solution.py:18
  172.1 11.7 %fusion.27 = f32[32,8192]{1,0:T(8,128)} fusion(bf16[32,1280]{1,0:T(8,128)(2,1)S(1)} %fusion.19, bf16[1280,8192]{1,0:T(8,128)(2,1)} %param.30), kind=kOutput, calls=%fused_computation.45 | convolution fusion | flops 671088640 | bytes 22102016 | tf_op jit(solution)/shard_map/dot_general | solution.py:118
  183.9 59.3 %reduce-scatter.2.cloned.1.call-done = f32[32,512]{1,0:T(8,128)} async-done(((f32[32,8192]{1,0:T(8,128)}), f32[32,512]{1,0:T(8,128)}) %reduce-scatter.2.cloned.1.call-update) | async-done | bytes 65552 | tf_op jit(solution)/shard_map/reduce_scatter | solution.py:119
  (91 shorter events, 52.1 us)
Async XLA Ops:
  6.5 2.2 copy-start
  6.5 236.6 %reduce-scatter.2.cloned.1.call-start = ((), (), s32[]{:S(2)}) async-start(), calls=%async_computation.1 | async-start | bytes 1114112 | tf_op jit(solution)/shard_map/reduce_scatter | solution.py:119
  161.6 83.0 %copy-start.1 = (bf16[1,16,128]{2,1,0:T(8,128)(2,1)S(1)}, bf16[1,16,128]{2,1,0:T(8,128)(2,1)}, u32[]{:S(2)}) copy-start(bf16[1,16,128]{2,1,0:T(8,128)(2,1)} %param.22) | copy-start | bytes 12292
  172.1 71.0 %copy-start.2 = (bf16[32,512]{1,0:T(8,128)(2,1)S(1)}, bf16[32,512]{1,0:T(8,128)(2,1)}, u32[]{:S(2)}) copy-start(bf16[32,512]{1,0:T(8,128)(2,1)} %param.26) | copy-start | bytes 98308
Sparse Core Ops, SparseCore 0:
  184.0 59.0 reduce-scatter.1
where the time goes:
time: 253 us; the launch traced here: 251 us
  matrix products  77.6 us (31%)
  blocking collectives  70.1 us (28%)
  waiting for transfers between devices  59.3 us (23%)
  other arithmetic  29.4 us (12%)
  between operations  14.2 us (6%)
    reduce_scatter x1, waiting for transfers between devices, on_device(): lax.psum_scatter(down_terms, 'wide', scatter_dimension=1, tiled=True)  59.3 us
    dot_general x18, matrix products, contract_last(): lax.dot_general(left, right, (((1,), (1,)), ((), ())), preferred_element_...  46.5 us
    psum x1, blocking collectives, on_device(): row_squares = lax.psum(jnp.sum(hidden_state * hidden_state, axis=1), 'wide')  29.8 us
    all_gather x1, blocking collectives, on_device(): head_piece = lax.all_gather(attended, 'wide', axis=0, tiled=True)  21.5 us
    all_gather x1, blocking collectives, on_device(): normed_piece = lax.all_gather(normed_cols, 'wide', axis=1, tiled=True)  18.8 us
    dot_general x10, matrix products, masked_scores(): jnp.einsum('rqe,rpe->rqp', query_rows, key_block, preferred_element_type=...  12.9 us
    scatter-add x16, other arithmetic, one_source(): return running.at[request_ids].add(term)  12 us
    select_n x16, other arithmetic, one_source(): return running.at[request_ids].add(term)  11.7 us
  transfers between devices with their start and end apart: 1, of which 1 were waited for; matrix products, arithmetic and copies ran while one was open for 0% of the time, Pallas kernels for 0%

commit v1 on v0

--- a/solution.py
+++ b/solution.py
@@ -1,8 +1,11 @@
+import functools
 import math
 
 import jax
 import jax.numpy as jnp
 from jax import lax
+from jax.experimental import pallas as pl
+from jax.experimental.pallas import tpu as pltpu
 from jax.sharding import PartitionSpec as P
 
 D = 8192
@@ -28,6 +31,420 @@
     )
     position = block_index * KEY_BLOCK + lax.broadcasted_iota(jnp.int32, scores.shape, 2)
     return jnp.where(position < lens_local[:, None, None], scores, NEG_FILL)
+
+
+SLOT_COUNT = 44
+VMEM_BYTES = 67043328
+
+
+def layer_kernel(
+    n,
+    lengths,
+    assignment,
+    queries,
+    new_keys,
+    new_values,
+    residual,
+    norm_gain,
+    keys_hbm,
+    values_hbm,
+    w_out,
+    w_gate,
+    w_up,
+    w_down,
+    out,
+    keys,
+    values,
+    slots,
+    scores,
+    weights,
+    acc,
+    heads,
+    state,
+    scaled,
+    squares,
+    gate_acc,
+    up_acc,
+    hidden,
+    send_parts,
+    recv_parts,
+    own_part,
+    cache_sems,
+    slot_sems,
+    head_send,
+    head_recv,
+    scaled_send,
+    scaled_recv,
+    square_send,
+    square_recv,
+    part_send,
+    part_recv,
+):
+    me = lax.axis_index("wide")
+    my_shard, my_group = me // KV, me % KV
+    req_dev, qpk, head = queries.shape[1:]
+    requests, cols = residual.shape
+    units = w_gate.shape[0]
+    shards = n // KV
+    halves = qpk * head // cols
+    extra = SLOT_COUNT - KV - 2 * n
+
+    def source(k):
+        return lax.rem(me - k + n, n)
+
+    def target(k):
+        return lax.rem(me + k, n)
+
+    def col_block(index):
+        return pl.ds(pl.multiple_of(index * cols, cols), cols)
+
+    def out_fill(k, half):
+        group = lax.rem(my_group - k + KV, KV)
+        return pltpu.make_async_copy(
+            w_out.at[:, col_block(group * halves + half)],
+            slots.at[k, pl.ds(half * cols, cols)],
+            slot_sems.at[k, half],
+        )
+
+    def gate_fill(k):
+        slot = KV + 2 * k
+        return pltpu.make_async_copy(
+            w_gate.at[:, col_block(source(k))], slots.at[slot], slot_sems.at[slot, 0]
+        )
+
+    def up_fill(k):
+        slot = KV + 2 * k + 1
+        return pltpu.make_async_copy(
+            w_up.at[:, col_block(source(k))], slots.at[slot], slot_sems.at[slot, 0]
+        )
+
+    def down_slot(k):
+        return jnp.where(k < extra, KV + 2 * n + k, k - extra)
+
+    def down_fill(k):
+        slot = down_slot(k)
+        return pltpu.make_async_copy(
+            w_down.at[:, col_block(target(k + 1))], slots.at[slot], slot_sems.at[slot, 0]
+        )
+
+    def remote(src, dst, send_sem, recv_sem, device):
+        return pltpu.make_async_remote_copy(
+            src_ref=src,
+            dst_ref=dst,
+            send_sem=send_sem,
+            recv_sem=recv_sem,
+            device_id={"wide": device},
+            device_id_type=pl.DeviceIdType.MESH,
+        )
+
+    def head_copy(k, owner):
+        return remote(
+            heads.at[owner], heads.at[owner], head_send.at[k], head_recv.at[owner], target(k)
+        )
+
+    def scaled_copy(k, owner):
+        return remote(
+            scaled.at[owner], scaled.at[owner], scaled_send.at[k], scaled_recv.at[owner], target(k)
+        )
+
+    def square_copy(k, owner):
+        return remote(
+            squares.at[owner],
+            squares.at[owner],
+            square_send.at[k],
+            square_recv.at[owner],
+            target(k),
+        )
+
+    def part_copy(k, owner):
+        return remote(
+            send_parts.at[k], recv_parts.at[owner], part_send.at[k], part_recv.at[owner], target(k)
+        )
+
+    def each(low, high, body):
+        def step(k, carry):
+            body(k)
+            return carry
+
+        lax.fori_loop(low, high, step, 0)
+
+    key_copy = pltpu.make_async_copy(keys_hbm.at[0], keys, cache_sems.at[0])
+    value_copy = pltpu.make_async_copy(values_hbm.at[0], values, cache_sems.at[1])
+    key_copy.start()
+    value_copy.start()
+
+    @functools.partial(each, 0, KV)
+    def _(k):
+        for half in range(halves):
+            out_fill(k, half).start()
+
+    barrier = pltpu.get_barrier_semaphore()
+
+    @functools.partial(each, 1, n)
+    def _(k):
+        pl.semaphore_signal(
+            barrier,
+            inc=1,
+            device_id={"wide": target(k)},
+            device_id_type=pl.DeviceIdType.MESH,
+        )
+
+    key_copy.wait()
+    value_copy.wait()
+
+    @functools.partial(each, 0, n)
+    def _(k):
+        gate_fill(k).start()
+        up_fill(k).start()
+
+    @functools.partial(each, 0, min(extra, n))
+    def _(k):
+        down_fill(k).start()
+
+    inv_scale = 1.0 / math.sqrt(head)
+    for row in range(req_dev):
+        block = contract_last(queries[0, row], keys[row]) * inv_scale
+        position = lax.broadcasted_iota(jnp.int32, block.shape, 1)
+        scores[row] = jnp.where(
+            position < lengths[my_shard * req_dev + row], block, NEG_FILL
+        )
+    own_score = (
+        jnp.sum(
+            queries[0].astype(jnp.float32) * new_keys[0].astype(jnp.float32)[:, None, :],
+            axis=2,
+            keepdims=True,
+        )
+        * inv_scale
+    )
+    all_scores = scores[...]
+    top = jnp.maximum(jnp.max(all_scores, axis=2, keepdims=True), own_score)
+    exps = jnp.exp(all_scores - top)
+    own_weight = jnp.exp(own_score - top)
+    total = jnp.sum(exps, axis=2, keepdims=True) + own_weight
+    weights[...] = exps.astype(jnp.bfloat16)
+    for row in range(req_dev):
+        acc[row] = jnp.dot(weights[row], values[row], preferred_element_type=jnp.float32)
+    own_low = own_weight.astype(jnp.bfloat16).astype(jnp.float32)
+    own_term = own_low * new_values[0].astype(jnp.float32)[:, None, :]
+    acc[...] = (acc[...] + own_term) / total
+    for index in range(qpk):
+        heads[me, :, index * head : (index + 1) * head] = acc[:, index, :].astype(jnp.bfloat16)
+
+    pl.semaphore_wait(barrier, n - 1)
+
+    @functools.partial(each, 1, n)
+    def _(k):
+        head_copy(k, me).start()
+
+    request_row = lax.broadcasted_iota(jnp.int32, (requests, requests), 0)
+    cache_col = lax.broadcasted_iota(jnp.int32, (requests, requests), 1)
+    place = jnp.zeros((requests, requests), jnp.float32)
+    for row in range(requests):
+        place = jnp.where(
+            jnp.logical_and(cache_col == row, request_row == assignment[row]), 1.0, place
+        )
+    state[...] = lax.dot_general(
+        place.T.astype(jnp.bfloat16),
+        residual[...],
+        (((1,), (0,)), ((), ())),
+        preferred_element_type=jnp.float32,
+    )
+
+    @functools.partial(each, 0, KV)
+    def _(k):
+        group = lax.rem(my_group - k + KV, KV)
+        for half in range(halves):
+            out_fill(k, half).wait()
+        for shard in range(shards):
+            owner = shard * KV + group
+
+            @pl.when(owner != me)
+            def _():
+                head_copy(0, owner).wait_recv()
+
+        rows = jnp.concatenate([heads[shard * KV + group] for shard in range(shards)], axis=0)
+        term = state[...]
+        for half in range(halves):
+            term = term + contract_last(
+                rows[:, half * cols : (half + 1) * cols],
+                slots[k, half * cols : (half + 1) * cols, :],
+            )
+        state[...] = term
+
+    my_state = state[...]
+    scaled[me] = (my_state * norm_gain[...][None, :]).astype(jnp.bfloat16)
+    row_sums = jnp.sum(my_state * my_state, axis=1, keepdims=True)
+    diagonal = lax.broadcasted_iota(
+        jnp.int32, (requests, squares.shape[2]), 0
+    ) == lax.broadcasted_iota(jnp.int32, (requests, squares.shape[2]), 1)
+    flat_sums = jnp.sum(jnp.where(diagonal, row_sums, 0.0), axis=0, keepdims=True)
+    squares[me] = jnp.broadcast_to(flat_sums, squares.shape[1:])
+
+    @functools.partial(each, 1, n)
+    def _(k):
+        scaled_copy(k, me).start()
+        square_copy(k, me).start()
+
+    @functools.partial(each, extra, min(extra + KV, n))
+    def _(k):
+        down_fill(k).start()
+
+    gate_acc[...] = jnp.zeros_like(gate_acc)
+    up_acc[...] = jnp.zeros_like(up_acc)
+
+    @functools.partial(each, 0, n)
+    def _(k):
+        owner = source(k)
+        gate_fill(k).wait()
+        up_fill(k).wait()
+
+        @pl.when(k > 0)
+        def _():
+            scaled_copy(0, owner).wait_recv()
+
+        piece = scaled[owner]
+        gate_acc[...] += contract_last(piece, slots[KV + 2 * k])
+        up_acc[...] += contract_last(piece, slots[KV + 2 * k + 1])
+
+        for step in range(2):
+            later = extra + KV + 2 * k + step
+
+            @pl.when(later < n)
+            def _():
+                down_fill(later).start()
+
+    @functools.partial(each, 1, n)
+    def _(k):
+        square_copy(0, source(k)).wait_recv()
+
+    sum_squares = jnp.sum(squares[...], axis=0)[:1]
+    row_squares = jnp.sum(jnp.where(diagonal, sum_squares, 0.0), axis=1, keepdims=True)
+    inv_rms = lax.rsqrt(row_squares / (n * cols) + EPSILON)
+    gate_val = gate_acc[...] * inv_rms
+    hidden[...] = (gate_val * jax.nn.sigmoid(gate_val) * (up_acc[...] * inv_rms)).astype(
+        jnp.bfloat16
+    )
+
+    @functools.partial(each, 0, n)
+    def _(k):
+        down_fill(k).wait()
+        part = jnp.dot(hidden[...], slots[down_slot(k)], preferred_element_type=jnp.float32)
+
+        @pl.when(k < n - 1)
+        def _():
+            send_parts[k + 1] = part.astype(jnp.bfloat16)
+            part_copy(k + 1, me).start()
+
+        @pl.when(k == n - 1)
+        def _():
+            own_part[...] = part + state[...]
+
+    @functools.partial(each, 1, n)
+    def _(k):
+        owner = source(k)
+        part_copy(0, owner).wait_recv()
+        own_part[...] += recv_parts[owner].astype(jnp.float32)
+
+    out[...] = jnp.dot(
+        place.astype(jnp.bfloat16),
+        own_part[...].astype(jnp.bfloat16),
+        preferred_element_type=jnp.float32,
+    ).astype(jnp.bfloat16)
+
+    @functools.partial(each, 1, n)
+    def _(k):
+        head_copy(k, me).wait_send()
+        scaled_copy(k, me).wait_send()
+        square_copy(k, me).wait_send()
+        part_copy(k, me).wait_send()
+
+
+def kernel_fits(n, queries, keys_cache, residual, w_gate):
+    requests, cols = residual.shape
+    units = w_gate.shape[0]
+    feats = queries.shape[2] * queries.shape[3]
+    slot_bytes = SLOT_COUNT * units * cols * 2
+    return (
+        n % KV == 0
+        and cols % 128 == 0
+        and units % 128 == 0
+        and feats % cols == 0
+        and feats <= units
+        and requests <= 128
+        and KV + 2 * n <= SLOT_COUNT
+        and slot_bytes + 4 * keys_cache.size + (6 << 20) <= VMEM_BYTES
+    )
+
+
+def fused_layer(
+    n,
+    queries,
+    keys_cache,
+    values_cache,
+    new_keys,
+    new_values,
+    lengths,
+    assignment,
+    residual,
+    w_out,
+    w_gate,
+    w_up,
+    w_down,
+    norm_gain,
+):
+    req_dev, qpk, head = queries.shape[1:]
+    positions = keys_cache.shape[2]
+    requests, cols = residual.shape
+    units = w_gate.shape[0]
+    low, full = jnp.bfloat16, jnp.float32
+    smem = pl.BlockSpec(memory_space=pltpu.SMEM)
+    vmem = pl.BlockSpec(memory_space=pltpu.VMEM)
+    anywhere = pl.BlockSpec(memory_space=pl.ANY)
+    dma = pltpu.SemaphoreType.DMA
+    return pl.pallas_call(
+        functools.partial(layer_kernel, n),
+        out_shape=jax.ShapeDtypeStruct((requests, cols), low),
+        in_specs=[smem] * 2 + [vmem] * 5 + [anywhere] * 6,
+        out_specs=vmem,
+        scratch_shapes=[
+            pltpu.VMEM((req_dev, positions, head), low),
+            pltpu.VMEM((req_dev, positions, head), low),
+            pltpu.VMEM((SLOT_COUNT, units, cols), low),
+            pltpu.VMEM((req_dev, qpk, positions), full),
+            pltpu.VMEM((req_dev, qpk, positions), low),
+            pltpu.VMEM((req_dev, qpk, head), full),
+            pltpu.VMEM((n, req_dev, qpk * head), low),
+            pltpu.VMEM((requests, cols), full),
+            pltpu.VMEM((n, requests, cols), low),
+            pltpu.VMEM((n, 8, 128), full),
+            pltpu.VMEM((requests, units), full),
+            pltpu.VMEM((requests, units), full),
+            pltpu.VMEM((requests, units), low),
+            pltpu.VMEM((n, requests, cols), low),
+            pltpu.VMEM((n, requests, cols), low),
+            pltpu.VMEM((requests, cols), full),
+            dma((2,)),
+            dma((SLOT_COUNT, max(2, qpk * head // cols))),
+        ]
+        + [dma((n,))] * 8,
+        compiler_params=pltpu.CompilerParams(
+            collective_id=0, has_side_effects=True, vmem_limit_bytes=VMEM_BYTES
+        ),
+    )(
+        lengths,
+        assignment,
+        queries,
+        new_keys,
+        new_values,
+        residual,
+        norm_gain,
+        keys_cache,
+        values_cache,
+        w_out,
+        w_gate,
+        w_up,
+        w_down,
+    )
 
 
 def on_device(
@@ -45,6 +462,24 @@
     w_down,
     norm_gain,
 ):
+    n = lax.axis_size("wide")
+    if kernel_fits(n, queries, keys_cache, residual, w_gate):
+        return fused_layer(
+            n,
+            queries,
+            keys_cache,
+            values_cache,
+            new_keys,
+            new_values,
+            lengths,
+            assignment,
+            residual,
+            w_out,
+            w_gate,
+            w_up,
+            w_down,
+            norm_gain,
+        )
     my_index = lax.axis_index("wide")
     my_shard = my_index // KV
     req_dev = queries.shape[1]

time: 253 us -> 58.5 us (0.23)
  the two profiles are of different devices: /device:TPU:0 before, /device:TPU:13 now
where the time goes in v1:
time: 58.5 us; the launch traced here: 58.3 us
  Pallas kernels  56.9 us (97%)
  local copies, waits for them, and re-layouts  1.38 us (2%)
    pallas_call x1, Pallas kernels, fused_layer(): pl.pallas_call(functools.partial(layer_kernel, n), out_shape=jax.ShapeDty...  56.9 us
    unnamed x1, local copies, waits for them, and re-layouts  1.38 us

profile of v1, /device:TPU:13, one launch (start us, length us, event | category | flops | bytes accessed | tf_op | source)
XLA Modules:
  0.0 58.3 jit_solution(17745912168157802391)
XLA Ops:
  0.0 56.9 %shard_map.127 = bf16[32,512]{1,0:T(8,128)(2,1)} custom-call(s32[32]{0:T(128)} %lengths.1, s32[32]{0:T(128)} %assignment.1, bf16[1,16,8,128]{3,2,1,0:T(8,128)(2,1)} %queries.1, bf16[1,16,128]{2,1,0:T(8,128)(2,1)} %new_keys.1, bf16[1,16,128]{2,1,0:T(8,128)(2,1)} %new_values.1, bf16[32,512]{1,0:T(8,128)(2,1)} %residual.1, f32[512]{0:T(512)} %norm_gain.1, ...), custom_call_target="tpu_custom_call" | custom-call | tf_op jit(solution)/shard_map/pallas_call | solution.py:404
  56.9 1.4 %copy.15 = bf16[32,512]{1,0:T(8,128)(2,1)} copy(bf16[32,512]{1,0:T(8,128)(2,1)} %shard_map.127) | data formatting | bytes 65536
